TPU v7x, 512 devices: a whole 4x4x16 slice. The times are simulated.
512 devices in a mesh: gx: 8 (over y, core), gy: 4 (over x), gz: 16 (over z).
Axes of the slice: x: 4, y: 4, z: 16, core: 2. Of those that a mesh axis runs over, the one named last changes fastest.
Arguments:
- level_set: float32 [128, 64, 2048], P('gx', 'gy', 'gz'), may hold values from 0 to 1
- velocity: float32 [3, 128, 64, 2048], P(None, 'gx', 'gy', 'gz'), may hold values from -6 to 6
- source: float32 [128, 64, 2048], P('gx', 'gy', 'gz'), may hold values from -6 to 6
- coarse_factor: float32 [512, 512], P(('gx', 'gy', 'gz')), may hold values from -0.2 to 0.2
Outputs:
- level_set_new: float32 [128, 64, 2048], P('gx', 'gy', 'gz')
- pressure: float32 [128, 64, 2048], P('gx', 'gy', 'gz')
All inputs are finite; a program needn't handle non-finite values.
Results may differ from a plain program's by a relative error of at most 0.029.
Values sent between devices are 32-bit elements; how exact they have to be, the bound alone decides.
A program may use at most 64 MiB of HBM per device.

v0:
```python
import jax
import jax.numpy as jnp
import numpy as np
from jax import lax
from jax.sharding import PartitionSpec as P

NP = 8
RSWEEPS = 2
ITERS = 6
GLL_POINTS = (
    -1.0,
    -0.8717401485096066,
    -0.5917001814331423,
    -0.2092992179024789,
    0.2092992179024789,
    0.5917001814331423,
    0.8717401485096066,
    1.0,
)
GLL_WEIGHTS = (
    0.03571428571428571,
    0.21070422714350603,
    0.3411226924835044,
    0.4124587946587038,
    0.4124587946587038,
    0.3411226924835044,
    0.21070422714350603,
    0.03571428571428571,
)
HIGHEST = lax.Precision.HIGHEST
TIME_STEP = 0.02
PSEUDO_STEP = 0.004
INTERFACE_WIDTH = 0.5
GAS_DENSITY = 0.1
SOURCE_SCALE = 20.0


def extended(cells, sides, width):
    for axis, dim in sides:
        count = lax.axis_size(axis)
        ends = count - 1
        head = lax.slice_in_dim(cells, 0, width, axis=dim)
        tail = lax.slice_in_dim(cells, cells.shape[dim] - width, cells.shape[dim], axis=dim)
        cells = jnp.concatenate(
            [
                lax.ppermute(tail, axis, [(i, (i + 1) % count) for i in range(ends)]),
                cells,
                lax.ppermute(head, axis, [((i + 1) % count, i) for i in range(ends)]),
            ],
            axis=dim,
        )
    return cells


def node_tables():
    points = np.array(GLL_POINTS)
    amount = points.shape[0]
    barycentric = np.ones(amount)
    for target in range(amount):
        for partner in range(amount):
            if partner != target:
                barycentric[target] = barycentric[target] / (points[target] - points[partner])
    derivative = np.zeros((amount, amount))
    for target in range(amount):
        for partner in range(amount):
            if partner != target:
                derivative[target, partner] = (
                    barycentric[partner] / barycentric[target] / (points[target] - points[partner])
                )
        derivative[target, target] = -np.sum(derivative[target])
    return derivative


def apply_axis(values, matrix, which_axis):
    if which_axis == 0:
        return jnp.einsum("ap,pqr->aqr", matrix, values, precision=HIGHEST)
    if which_axis == 1:
        return jnp.einsum("aq,pqr->par", matrix, values, precision=HIGHEST)
    return jnp.einsum("pqr,ar->pqa", values, matrix, precision=HIGHEST)


def edge_passes(padded):
    summed = padded
    for which_axis in (1, 2, 3):
        amount = summed.shape[which_axis] - 2
        center = lax.slice_in_dim(summed, 1, amount + 1, axis=which_axis)
        upper_side = lax.slice_in_dim(summed, 2, amount + 2, axis=which_axis)
        lower_side = lax.slice_in_dim(summed, 0, amount, axis=which_axis)
        shape_list = [1, 1, 1, 1]
        shape_list[which_axis] = amount
        position = (jnp.arange(amount) % NP).reshape(shape_list)
        summed = (
            center
            + jnp.where(position == NP - 1, upper_side, 0.0)
            + jnp.where(position == 0, lower_side, 0.0)
        )
    return summed


def assemble(stacked):
    padded = extended(stacked, (("gx", 1), ("gy", 2), ("gz", 3)), 1)
    return edge_passes(padded)


def body(level_set, velocity, source, coarse_factor):
    shape_tuple = level_set.shape
    derivative = node_tables()
    deriv_tables = [
        jnp.asarray(np.kron(np.eye(extent // NP), derivative), jnp.float32)
        for extent in shape_tuple
    ]
    trans_tables = [
        jnp.asarray(np.kron(np.eye(extent // NP), derivative.T), jnp.float32)
        for extent in shape_tuple
    ]
    square_tables = [
        jnp.asarray(np.kron(np.eye(extent // NP), (derivative * derivative).T), jnp.float32)
        for extent in shape_tuple
    ]
    weights = jnp.asarray(np.array(GLL_WEIGHTS), jnp.float32)
    along_x = jnp.tile(weights, shape_tuple[0] // NP)
    along_y = jnp.tile(weights, shape_tuple[1] // NP)
    along_z = jnp.tile(weights, shape_tuple[2] // NP)
    bmass = along_x[:, None, None] * along_y[None, :, None] * along_z[None, None, :]
    gradient = [
        apply_axis(level_set, deriv_tables[which_axis], which_axis) for which_axis in range(3)
    ]
    advect = velocity[0] * gradient[0] + velocity[1] * gradient[1] + velocity[2] * gradient[2]
    divergence = (
        apply_axis(bmass * velocity[0], trans_tables[0], 0)
        + apply_axis(bmass * velocity[1], trans_tables[1], 1)
        + apply_axis(bmass * velocity[2], trans_tables[2], 2)
        + bmass * source
    )
    assembled = assemble(jnp.stack([bmass * advect, bmass, divergence]))
    mass_sum = assembled[1]
    weight = bmass / mass_sum
    level_now = level_set - TIME_STEP * assembled[0] / mass_sum
    rhs_field = SOURCE_SCALE * assembled[2]
    for sweep in range(RSWEEPS):
        gradient = [
            apply_axis(level_now, deriv_tables[which_axis], which_axis) for which_axis in range(3)
        ]
        inv_norm = 1.0 / jnp.sqrt(
            1.0 + gradient[0] * gradient[0] + gradient[1] * gradient[1] + gradient[2] * gradient[2]
        )
        compress = level_now * (1.0 - level_now) * inv_norm
        weak_form = apply_axis(
            bmass * (compress * gradient[0] - INTERFACE_WIDTH * gradient[0]), trans_tables[0], 0
        )
        weak_form = weak_form + apply_axis(
            bmass * (compress * gradient[1] - INTERFACE_WIDTH * gradient[1]), trans_tables[1], 1
        )
        weak_form = weak_form + apply_axis(
            bmass * (compress * gradient[2] - INTERFACE_WIDTH * gradient[2]), trans_tables[2], 2
        )
        level_now = level_now + PSEUDO_STEP * assemble(weak_form[None])[0] / mass_sum
    inverse_density = 1.0 / (GAS_DENSITY + (1.0 - GAS_DENSITY) * jnp.clip(level_now, 0.0, 1.0))
    scaled = bmass * inverse_density
    diag_local = (
        apply_axis(scaled, square_tables[0], 0)
        + apply_axis(scaled, square_tables[1], 1)
        + apply_axis(scaled, square_tables[2], 2)
        + bmass
    )
    diagonal = assemble(diag_local[None])[0]
    own_row = coarse_factor[0]

    def precondition(residual):
        jacobi = residual / diagonal
        restricted = jnp.sum(weight * residual)
        coarse_mid = lax.psum(restricted * own_row, ("gx", "gy", "gz"))
        coarse_value = jnp.dot(own_row, coarse_mid, precision=HIGHEST)
        result = jacobi + assemble((weight * coarse_value)[None])[0]
        return (result, lax.psum(jnp.sum(weight * residual * result), ("gx", "gy", "gz")))

    pressure = jnp.zeros_like(rhs_field)
    residual = rhs_field
    direction, inner_now = precondition(residual)
    for step in range(ITERS):
        local_part = bmass * direction
        for element_which_axis in range(3):
            local_part = local_part + apply_axis(
                scaled
                * apply_axis(direction, deriv_tables[element_which_axis], element_which_axis),
                trans_tables[element_which_axis],
                element_which_axis,
            )
        image = assemble(local_part[None])[0]
        curvature = lax.psum(jnp.sum(weight * direction * image), ("gx", "gy", "gz"))
        step_size = inner_now / curvature
        pressure = pressure + step_size * direction
        residual = residual - step_size * image
        if step + 1 < ITERS:
            preconditioned, inner_next = precondition(residual)
            direction = preconditioned + inner_next / inner_now * direction
            inner_now = inner_next
    return (level_now, pressure)


def solution(mesh):
    in_specs = (
        P("gx", "gy", "gz"),
        P(None, "gx", "gy", "gz"),
        P("gx", "gy", "gz"),
        P(("gx", "gy", "gz"), None),
    )
    out_specs = (P("gx", "gy", "gz"), P("gx", "gy", "gz"))
    return jax.shard_map(body, mesh=mesh, in_specs=in_specs, out_specs=out_specs, check_vma=False)
```

profile of v0, /device:TPU:1, one launch (start us, length us, event | category | flops | bytes accessed | tf_op | source)
XLA Modules:
  0.0 2206.5 jit_solution(12459862347474892173)
XLA Ops:
  6.2 4.6 collective-permute-start
  10.8 5.5 collective-permute-start.1
  63.5 5.4 collective-permute-done.11
  87.6 4.9 collective-permute-start.16
  103.5 104.3 %psum.126 = f32[512]{0:T(512)S(1)} all-reduce(f32[512]{0:T(512)S(1)} %broadcast_multiply_fusion.13), channel_id=1, replica_groups=mesh['gx'=8,'gy'=4,'gz'=16] {'gx','gy','gz'}, use_global_device_ids=true, to_apply=%region_1.2 | all-reduce | flops 512 | bytes 4096 | tf_op jit(solution)/shard_map/psum | solution.py:172
  240.6 4.4 collective-permute-done.23
  256.2 4.3 collective-permute-start.32
  273.4 4.8 collective-permute-done.35
  279.6 104.5 %all-reduce = (f32[]{:T(128)}, f32[]{:T(128)}) all-reduce(f32[]{:T(128)} %get-tuple-element.9, f32[]{:T(128)} %get-tuple-element.8), channel_id=1, replica_groups=mesh['gx'=8,'gy'=4,'gz'=16] {'gx','gy','gz'}, use_global_device_ids=true, to_apply=%region_3.4 | all-reduce | flops 2 | bytes 16 | tf_op jit(solution)/shard_map/psum | solution.py:175
  386.8 98.4 %psum.129 = f32[512]{0:T(512)S(1)} all-reduce(f32[512]{0:T(512)S(1)} %broadcast_multiply_fusion.12), channel_id=1, replica_groups=mesh['gx'=8,'gy'=4,'gz'=16] {'gx','gy','gz'}, use_global_device_ids=true, to_apply=%region_7.8 | all-reduce | flops 512 | bytes 4096 | tf_op jit(solution)/shard_map/psum | solution.py:172
  514.5 101.3 %psum.130 = f32[]{:T(128)} all-reduce(f32[]{:T(128)} %get-tuple-element.36), channel_id=1, replica_groups=mesh['gx'=8,'gy'=4,'gz'=16] {'gx','gy','gz'}, use_global_device_ids=true, to_apply=%region_9.10 | all-reduce | flops 1 | bytes 8 | tf_op jit(solution)/shard_map/psum | solution.py:175
  645.7 102.2 %psum.131 = f32[]{:T(128)} all-reduce(f32[]{:T(128)} %get-tuple-element.34), channel_id=1, replica_groups=mesh['gx'=8,'gy'=4,'gz'=16] {'gx','gy','gz'}, use_global_device_ids=true, to_apply=%region_11.12 | all-reduce | flops 1 | bytes 8 | tf_op jit(solution)/shard_map/psum | solution.py:190
  750.5 99.1 %psum.132 = f32[512]{0:T(512)S(1)} all-reduce(f32[512]{0:T(512)S(1)} %broadcast_multiply_fusion.11), channel_id=1, replica_groups=mesh['gx'=8,'gy'=4,'gz'=16] {'gx','gy','gz'}, use_global_device_ids=true, to_apply=%region_13.14 | all-reduce | flops 512 | bytes 4096 | tf_op jit(solution)/shard_map/psum | solution.py:172
  879.3 100.7 %psum.133 = f32[]{:T(128)} all-reduce(f32[]{:T(128)} %get-tuple-element.30), channel_id=1, replica_groups=mesh['gx'=8,'gy'=4,'gz'=16] {'gx','gy','gz'}, use_global_device_ids=true, to_apply=%region_15.16 | all-reduce | flops 1 | bytes 8 | tf_op jit(solution)/shard_map/psum | solution.py:175
  1009.8 102.3 %psum.134 = f32[]{:T(128)} all-reduce(f32[]{:T(128)} %get-tuple-element.28), channel_id=1, replica_groups=mesh['gx'=8,'gy'=4,'gz'=16] {'gx','gy','gz'}, use_global_device_ids=true, to_apply=%region_17.18 | all-reduce | flops 1 | bytes 8 | tf_op jit(solution)/shard_map/psum | solution.py:190
  1114.7 98.7 %psum.135 = f32[512]{0:T(512)S(1)} all-reduce(f32[512]{0:T(512)S(1)} %broadcast_multiply_fusion.10), channel_id=1, replica_groups=mesh['gx'=8,'gy'=4,'gz'=16] {'gx','gy','gz'}, use_global_device_ids=true, to_apply=%region_19.20 | all-reduce | flops 512 | bytes 4096 | tf_op jit(solution)/shard_map/psum | solution.py:172
  1243.1 100.7 %psum.136 = f32[]{:T(128)} all-reduce(f32[]{:T(128)} %get-tuple-element.24), channel_id=1, replica_groups=mesh['gx'=8,'gy'=4,'gz'=16] {'gx','gy','gz'}, use_global_device_ids=true, to_apply=%region_21.22 | all-reduce | flops 1 | bytes 8 | tf_op jit(solution)/shard_map/psum | solution.py:175
  1373.6 102.5 %psum.137 = f32[]{:T(128)} all-reduce(f32[]{:T(128)} %get-tuple-element.22), channel_id=1, replica_groups=mesh['gx'=8,'gy'=4,'gz'=16] {'gx','gy','gz'}, use_global_device_ids=true, to_apply=%region_23.24 | all-reduce | flops 1 | bytes 8 | tf_op jit(solution)/shard_map/psum | solution.py:190
  1478.7 98.7 %psum.138 = f32[512]{0:T(512)S(1)} all-reduce(f32[512]{0:T(512)S(1)} %broadcast_multiply_fusion.9), channel_id=1, replica_groups=mesh['gx'=8,'gy'=4,'gz'=16] {'gx','gy','gz'}, use_global_device_ids=true, to_apply=%region_25.26 | all-reduce | flops 512 | bytes 4096 | tf_op jit(solution)/shard_map/psum | solution.py:172
  1607.0 100.7 %psum.139 = f32[]{:T(128)} all-reduce(f32[]{:T(128)} %get-tuple-element.18), channel_id=1, replica_groups=mesh['gx'=8,'gy'=4,'gz'=16] {'gx','gy','gz'}, use_global_device_ids=true, to_apply=%region_27.28 | all-reduce | flops 1 | bytes 8 | tf_op jit(solution)/shard_map/psum | solution.py:175
  1737.5 102.3 %psum.140 = f32[]{:T(128)} all-reduce(f32[]{:T(128)} %get-tuple-element.16), channel_id=1, replica_groups=mesh['gx'=8,'gy'=4,'gz'=16] {'gx','gy','gz'}, use_global_device_ids=true, to_apply=%region_29.30 | all-reduce | flops 1 | bytes 8 | tf_op jit(solution)/shard_map/psum | solution.py:190
  1842.5 98.7 %psum.141 = f32[512]{0:T(512)S(1)} all-reduce(f32[512]{0:T(512)S(1)} %broadcast_multiply_fusion.8), channel_id=1, replica_groups=mesh['gx'=8,'gy'=4,'gz'=16] {'gx','gy','gz'}, use_global_device_ids=true, to_apply=%region_31.32 | all-reduce | flops 512 | bytes 4096 | tf_op jit(solution)/shard_map/psum | solution.py:172
  1970.8 100.7 %psum.142 = f32[]{:T(128)} all-reduce(f32[]{:T(128)} %get-tuple-element.12), channel_id=1, replica_groups=mesh['gx'=8,'gy'=4,'gz'=16] {'gx','gy','gz'}, use_global_device_ids=true, to_apply=%region_33.34 | all-reduce | flops 1 | bytes 8 | tf_op jit(solution)/shard_map/psum | solution.py:175
  2102.2 102.1 %psum.143 = f32[]{:T(128)} all-reduce(f32[]{:T(128)} %fusion.92), channel_id=1, replica_groups=mesh['gx'=8,'gy'=4,'gz'=16] {'gx','gy','gz'}, use_global_device_ids=true, to_apply=%region_35.36 | all-reduce | flops 1 | bytes 8 | tf_op jit(solution)/shard_map/psum | solution.py:190
  (437 shorter events, 436.9 us)
Async XLA Ops:
  6.2 10.1 collective-permute-start
  54.7 8.8 collective-permute-start.10
  58.3 10.6 collective-permute-start.11
  87.6 10.1 collective-permute-start.16
  92.5 9.1 collective-permute-start.17
  209.1 10.4 collective-permute-start.24
  214.4 8.8 collective-permute-start.18
  219.6 9.2 collective-permute-start.26
  231.8 8.8 collective-permute-start.22
  235.7 9.3 collective-permute-start.23
  268.2 10.0 collective-permute-start.35
  500.5 8.7 collective-permute-start.40
  504.2 8.9 collective-permute-start.41
  635.3 9.1 collective-permute-start.47
  865.3 8.7 collective-permute-start.52
  869.0 8.9 collective-permute-start.53
  999.4 9.1 collective-permute-start.59
  1229.1 8.7 collective-permute-start.64
  1232.8 8.9 collective-permute-start.65
  1363.2 9.1 collective-permute-start.71
  1596.8 8.9 collective-permute-start.77
  1727.1 9.1 collective-permute-start.83
  1960.6 8.9 collective-permute-start.89
  2091.0 9.1 collective-permute-start.95
  (81 other events, 617.3 us)
where the time goes:
time: 2220 us; the launch traced here: 2210 us
  blocking collectives  1720 us (77%)
  starting transfers between devices  211 us (10%)
  waiting for transfers between devices  199 us (9%)
  other arithmetic  36.4 us (2%)
    psum x6, blocking collectives, precondition(): lax.psum(jnp.sum(weight * residual * result), ('gx', 'gy', 'gz'))  609 us
    psum x6, blocking collectives, precondition(): coarse_mid = lax.psum(restricted * own_row, ('gx', 'gy', 'gz'))  598 us
    psum x5, blocking collectives, body(): lax.psum(jnp.sum(weight * direction * image), ('gx', 'gy', 'gz'))  511 us
    ppermute x48, waiting for transfers between devices, extended(): lax.ppermute(head, axis, [((i + 1) % count, i) for i in range(ends)])  147 us
    ppermute x48, starting transfers between devices, extended(): lax.ppermute(tail, axis, [(i, (i + 1) % count) for i in range(ends)])  133 us
    ppermute x48, starting transfers between devices, extended(): lax.ppermute(head, axis, [((i + 1) % count, i) for i in range(ends)])  77.4 us
    ppermute x48, waiting for transfers between devices, extended(): lax.ppermute(tail, axis, [(i, (i + 1) % count) for i in range(ends)])  51.5 us
  transfers between devices with their start and end apart: 96, of which 59 were waited for; matrix products, arithmetic and copies ran while one was open for 0% of the time, Pallas kernels for 0%

commit v1 on v0

--- a/solution.py
+++ b/solution.py
@@ -169,7 +169,7 @@
     def precondition(residual):
         jacobi = residual / diagonal
         restricted = jnp.sum(weight * residual)
-        coarse_mid = lax.psum(restricted * own_row, ("gx", "gy", "gz"))
+        coarse_mid = lax.psum(lax.psum(restricted * own_row, "gx"), ("gy", "gz"))
         coarse_value = jnp.dot(own_row, coarse_mid, precision=HIGHEST)
         result = jacobi + assemble((weight * coarse_value)[None])[0]
         return (result, lax.psum(jnp.sum(weight * residual * result), ("gx", "gy", "gz")))

time: 2220 us -> 2490 us (1.12)
  starting transfers between devices: 211 us -> 370 us
  blocking collectives: 1720 us -> 1840 us
    ppermute x48, starting transfers between devices: 133 us -> 289 us  [extended(): lax.ppermute(tail, axis, [(i, (i + 1) % count) for i in range(ends)])]
    psum x6 -> x12, blocking collectives: 598 us -> 747 us  [precondition(): coarse_mid = lax.psum(lax.psum(restricted * own_row, 'gx'), ('gy', 'gz'))]
  transfers between devices with their start and end apart: 96 -> 96, of which waited for: 59 -> 60; matrix products, arithmetic and copies ran while one was open for 0% -> 0% of each run, Pallas kernels for 0% -> 0%
where the time goes in v1:
time: 2490 us; the launch traced here: 2480 us
  blocking collectives  1840 us (74%)
  starting transfers between devices  370 us (15%)
  waiting for transfers between devices  190 us (8%)
  other arithmetic  36.4 us (1%)
    psum x12, blocking collectives, precondition(): coarse_mid = lax.psum(lax.psum(restricted * own_row, 'gx'), ('gy', 'gz'))  747 us
    psum x6, blocking collectives, precondition(): lax.psum(jnp.sum(weight * residual * result), ('gx', 'gy', 'gz'))  592 us
    psum x5, blocking collectives, body(): lax.psum(jnp.sum(weight * direction * image), ('gx', 'gy', 'gz'))  503 us
    ppermute x48, starting transfers between devices, extended(): lax.ppermute(tail, axis, [(i, (i + 1) % count) for i in range(ends)])  289 us
    ppermute x48, waiting for transfers between devices, extended(): lax.ppermute(head, axis, [((i + 1) % count, i) for i in range(ends)])  143 us
    ppermute x48, starting transfers between devices, extended(): lax.ppermute(head, axis, [((i + 1) % count, i) for i in range(ends)])  80.7 us
  transfers between devices with their start and end apart: 96, of which 60 were waited for; matrix products, arithmetic and copies ran while one was open for 0% of the time, Pallas kernels for 0%

profile of v1, /device:TPU:1, one launch (start us, length us, event | category | flops | bytes accessed | tf_op | source)
XLA Modules:
  0.0 2480.3 jit_solution(3534614058147929920)
XLA Ops:
  116.0 112.0 %psum.169 = f32[512]{0:T(512)S(1)} all-reduce(f32[512]{0:T(512)S(1)} %psum.168), channel_id=1, replica_groups=mesh['gx'=8,'gy'=4,'gz'=16] {'gy','gz'}, use_global_device_ids=true, to_apply=%region_2.3 | all-reduce | flops 512 | bytes 4096 | tf_op jit(solution)/shard_map/psum | solution.py:172
  229.3 29.3 %collective-permute-start.24 = (f32[1,1,16,128]{3,1,2,0:T(1,128)S(1)}, f32[1,1,16,128]{3,1,2,0:T(1,128)S(1)}, u32[]{:S(2)}, u32[]{:S(2)}) collective-permute-start(f32[1,1,16,128]{3,1,2,0:T(1,128)S(1)} %get-tuple-element.143), channel_id=1, source_target_pairs={{0,64},{64,128},{128,192},{192,256},{256,320},{320,384},{384,448},... | collective-permute-start | bytes 24584 | tf_op jit(solution)/shard_map/ppermute | solution.py:46
  323.7 99.5 %all-reduce = (f32[]{:T(128)}, f32[]{:T(128)}) all-reduce(f32[]{:T(128)} %get-tuple-element.9, f32[]{:T(128)} %get-tuple-element.8), channel_id=1, replica_groups=mesh['gx'=8,'gy'=4,'gz'=16] {'gx','gy','gz'}, use_global_device_ids=true, to_apply=%region_4.5 | all-reduce | flops 2 | bytes 16 | tf_op jit(solution)/shard_map/psum | solution.py:175
  425.9 12.4 psum.172
  438.3 112.7 %psum.173 = f32[512]{0:T(512)S(1)} all-reduce(f32[512]{0:T(512)S(1)} %psum.172), channel_id=1, replica_groups=mesh['gx'=8,'gy'=4,'gz'=16] {'gy','gz'}, use_global_device_ids=true, to_apply=%region_9.10 | all-reduce | flops 512 | bytes 4096 | tf_op jit(solution)/shard_map/psum | solution.py:172
  552.4 28.6 %collective-permute-start.36 = (f32[1,1,16,128]{3,1,2,0:T(1,128)S(1)}, f32[1,1,16,128]{3,1,2,0:T(1,128)S(1)}, u32[]{:S(2)}, u32[]{:S(2)}) collective-permute-start(f32[1,1,16,128]{3,1,2,0:T(1,128)S(1)} %get-tuple-element.137), channel_id=1, source_target_pairs={{0,64},{64,128},{128,192},{192,256},{256,320},{320,384},{384,448},... | collective-permute-start | bytes 24584 | tf_op jit(solution)/shard_map/ppermute | solution.py:46
  603.3 98.1 %psum.174 = f32[]{:T(128)} all-reduce(f32[]{:T(128)} %get-tuple-element.36), channel_id=1, replica_groups=mesh['gx'=8,'gy'=4,'gz'=16] {'gx','gy','gz'}, use_global_device_ids=true, to_apply=%region_11.12 | all-reduce | flops 1 | bytes 8 | tf_op jit(solution)/shard_map/psum | solution.py:175
  733.3 100.6 %psum.175 = f32[]{:T(128)} all-reduce(f32[]{:T(128)} %get-tuple-element.34), channel_id=1, replica_groups=mesh['gx'=8,'gy'=4,'gz'=16] {'gx','gy','gz'}, use_global_device_ids=true, to_apply=%region_13.14 | all-reduce | flops 1 | bytes 8 | tf_op jit(solution)/shard_map/psum | solution.py:190
  849.0 111.9 %psum.177 = f32[512]{0:T(512)S(1)} all-reduce(f32[512]{0:T(512)S(1)} %psum.176), channel_id=1, replica_groups=mesh['gx'=8,'gy'=4,'gz'=16] {'gy','gz'}, use_global_device_ids=true, to_apply=%region_16.17 | all-reduce | flops 512 | bytes 4096 | tf_op jit(solution)/shard_map/psum | solution.py:172
  962.3 28.9 %collective-permute-start.48 = (f32[1,1,16,128]{3,1,2,0:T(1,128)S(1)}, f32[1,1,16,128]{3,1,2,0:T(1,128)S(1)}, u32[]{:S(2)}, u32[]{:S(2)}) collective-permute-start(f32[1,1,16,128]{3,1,2,0:T(1,128)S(1)} %get-tuple-element.133), channel_id=1, source_target_pairs={{0,64},{64,128},{128,192},{192,256},{256,320},{320,384},{384,448},... | collective-permute-start | bytes 24584 | tf_op jit(solution)/shard_map/ppermute | solution.py:46
  1014.0 98.6 %psum.178 = f32[]{:T(128)} all-reduce(f32[]{:T(128)} %get-tuple-element.30), channel_id=1, replica_groups=mesh['gx'=8,'gy'=4,'gz'=16] {'gx','gy','gz'}, use_global_device_ids=true, to_apply=%region_18.19 | all-reduce | flops 1 | bytes 8 | tf_op jit(solution)/shard_map/psum | solution.py:175
  1144.2 100.6 %psum.179 = f32[]{:T(128)} all-reduce(f32[]{:T(128)} %get-tuple-element.28), channel_id=1, replica_groups=mesh['gx'=8,'gy'=4,'gz'=16] {'gx','gy','gz'}, use_global_device_ids=true, to_apply=%region_20.21 | all-reduce | flops 1 | bytes 8 | tf_op jit(solution)/shard_map/psum | solution.py:190
  1259.9 111.9 %psum.181 = f32[512]{0:T(512)S(1)} all-reduce(f32[512]{0:T(512)S(1)} %psum.180), channel_id=1, replica_groups=mesh['gx'=8,'gy'=4,'gz'=16] {'gy','gz'}, use_global_device_ids=true, to_apply=%region_23.24 | all-reduce | flops 512 | bytes 4096 | tf_op jit(solution)/shard_map/psum | solution.py:172
  1373.2 28.9 %collective-permute-start.60 = (f32[1,1,16,128]{3,1,2,0:T(1,128)S(1)}, f32[1,1,16,128]{3,1,2,0:T(1,128)S(1)}, u32[]{:S(2)}, u32[]{:S(2)}) collective-permute-start(f32[1,1,16,128]{3,1,2,0:T(1,128)S(1)} %get-tuple-element.129), channel_id=1, source_target_pairs={{0,64},{64,128},{128,192},{192,256},{256,320},{320,384},{384,448},... | collective-permute-start | bytes 24584 | tf_op jit(solution)/shard_map/ppermute | solution.py:46
  1424.9 98.4 %psum.182 = f32[]{:T(128)} all-reduce(f32[]{:T(128)} %get-tuple-element.24), channel_id=1, replica_groups=mesh['gx'=8,'gy'=4,'gz'=16] {'gx','gy','gz'}, use_global_device_ids=true, to_apply=%region_25.26 | all-reduce | flops 1 | bytes 8 | tf_op jit(solution)/shard_map/psum | solution.py:175
  1554.9 100.6 %psum.183 = f32[]{:T(128)} all-reduce(f32[]{:T(128)} %get-tuple-element.22), channel_id=1, replica_groups=mesh['gx'=8,'gy'=4,'gz'=16] {'gx','gy','gz'}, use_global_device_ids=true, to_apply=%region_27.28 | all-reduce | flops 1 | bytes 8 | tf_op jit(solution)/shard_map/psum | solution.py:190
  1670.6 111.9 %psum.185 = f32[512]{0:T(512)S(1)} all-reduce(f32[512]{0:T(512)S(1)} %psum.184), channel_id=1, replica_groups=mesh['gx'=8,'gy'=4,'gz'=16] {'gy','gz'}, use_global_device_ids=true, to_apply=%region_30.31 | all-reduce | flops 512 | bytes 4096 | tf_op jit(solution)/shard_map/psum | solution.py:172
  1783.9 28.9 %collective-permute-start.72 = (f32[1,1,16,128]{3,1,2,0:T(1,128)S(1)}, f32[1,1,16,128]{3,1,2,0:T(1,128)S(1)}, u32[]{:S(2)}, u32[]{:S(2)}) collective-permute-start(f32[1,1,16,128]{3,1,2,0:T(1,128)S(1)} %get-tuple-element.125), channel_id=1, source_target_pairs={{0,64},{64,128},{128,192},{192,256},{256,320},{320,384},{384,448},... | collective-permute-start | bytes 24584 | tf_op jit(solution)/shard_map/ppermute | solution.py:46
  1835.6 98.7 %psum.186 = f32[]{:T(128)} all-reduce(f32[]{:T(128)} %get-tuple-element.18), channel_id=1, replica_groups=mesh['gx'=8,'gy'=4,'gz'=16] {'gx','gy','gz'}, use_global_device_ids=true, to_apply=%region_32.33 | all-reduce | flops 1 | bytes 8 | tf_op jit(solution)/shard_map/psum | solution.py:175
  1965.9 100.6 %psum.187 = f32[]{:T(128)} all-reduce(f32[]{:T(128)} %get-tuple-element.16), channel_id=1, replica_groups=mesh['gx'=8,'gy'=4,'gz'=16] {'gx','gy','gz'}, use_global_device_ids=true, to_apply=%region_34.35 | all-reduce | flops 1 | bytes 8 | tf_op jit(solution)/shard_map/psum | solution.py:190
  2081.6 111.9 %psum.189 = f32[512]{0:T(512)S(1)} all-reduce(f32[512]{0:T(512)S(1)} %psum.188), channel_id=1, replica_groups=mesh['gx'=8,'gy'=4,'gz'=16] {'gy','gz'}, use_global_device_ids=true, to_apply=%region_37.38 | all-reduce | flops 512 | bytes 4096 | tf_op jit(solution)/shard_map/psum | solution.py:172
  2194.8 28.9 %collective-permute-start.84 = (f32[1,1,16,128]{3,1,2,0:T(1,128)S(1)}, f32[1,1,16,128]{3,1,2,0:T(1,128)S(1)}, u32[]{:S(2)}, u32[]{:S(2)}) collective-permute-start(f32[1,1,16,128]{3,1,2,0:T(1,128)S(1)} %get-tuple-element.121), channel_id=1, source_target_pairs={{0,64},{64,128},{128,192},{192,256},{256,320},{320,384},{384,448},... | collective-permute-start | bytes 24584 | tf_op jit(solution)/shard_map/ppermute | solution.py:46
  2246.5 98.4 %psum.190 = f32[]{:T(128)} all-reduce(f32[]{:T(128)} %get-tuple-element.12), channel_id=1, replica_groups=mesh['gx'=8,'gy'=4,'gz'=16] {'gx','gy','gz'}, use_global_device_ids=true, to_apply=%region_39.40 | all-reduce | flops 1 | bytes 8 | tf_op jit(solution)/shard_map/psum | solution.py:175
  2377.3 100.6 %psum.191 = f32[]{:T(128)} all-reduce(f32[]{:T(128)} %fusion.92), channel_id=1, replica_groups=mesh['gx'=8,'gy'=4,'gz'=16] {'gx','gy','gz'}, use_global_device_ids=true, to_apply=%region_41.42 | all-reduce | flops 1 | bytes 8 | tf_op jit(solution)/shard_map/psum | solution.py:190
  (443 shorter events, 509.2 us)
Async XLA Ops:
  6.2 10.1 collective-permute-start
  54.7 8.8 collective-permute-start.10
  58.3 10.6 collective-permute-start.11
  87.6 10.1 collective-permute-start.16
  92.5 9.1 collective-permute-start.17
  229.3 37.7 %collective-permute-start.24 = (f32[1,1,16,128]{3,1,2,0:T(1,128)S(1)}, f32[1,1,16,128]{3,1,2,0:T(1,128)S(1)}, u32[]{:S(2)}, u32[]{:S(2)}) collective-permute-start(f32[1,1,16,128]{3,1,2,0:T(1,128)S(1)} %get-tuple-element.143), channel_id=1, source_target_pairs={{0,64},{64,128},{128,192},{192,256},{256,320},{320,384},{384,448},... | collective-permute-start | bytes 24584 | tf_op jit(solution)/shard_map/ppermute | solution.py:46
  275.2 8.8 collective-permute-start.28
  276.7 9.2 collective-permute-start.29
  278.3 8.8 collective-permute-start.22
  313.3 9.1 collective-permute-start.35
  552.4 31.7 %collective-permute-start.36 = (f32[1,1,16,128]{3,1,2,0:T(1,128)S(1)}, f32[1,1,16,128]{3,1,2,0:T(1,128)S(1)}, u32[]{:S(2)}, u32[]{:S(2)}) collective-permute-start(f32[1,1,16,128]{3,1,2,0:T(1,128)S(1)} %get-tuple-element.137), channel_id=1, source_target_pairs={{0,64},{64,128},{128,192},{192,256},{256,320},{320,384},{384,448},... | collective-permute-start | bytes 24584 | tf_op jit(solution)/shard_map/ppermute | solution.py:46
  719.4 8.7 collective-permute-start.46
  723.1 8.9 collective-permute-start.47
  962.3 31.6 %collective-permute-start.48 = (f32[1,1,16,128]{3,1,2,0:T(1,128)S(1)}, f32[1,1,16,128]{3,1,2,0:T(1,128)S(1)}, u32[]{:S(2)}, u32[]{:S(2)}) collective-permute-start(f32[1,1,16,128]{3,1,2,0:T(1,128)S(1)} %get-tuple-element.133), channel_id=1, source_target_pairs={{0,64},{64,128},{128,192},{192,256},{256,320},{320,384},{384,448},... | collective-permute-start | bytes 24584 | tf_op jit(solution)/shard_map/ppermute | solution.py:46
  1130.3 8.7 collective-permute-start.58
  1134.0 8.9 collective-permute-start.59
  1373.2 31.6 %collective-permute-start.60 = (f32[1,1,16,128]{3,1,2,0:T(1,128)S(1)}, f32[1,1,16,128]{3,1,2,0:T(1,128)S(1)}, u32[]{:S(2)}, u32[]{:S(2)}) collective-permute-start(f32[1,1,16,128]{3,1,2,0:T(1,128)S(1)} %get-tuple-element.129), channel_id=1, source_target_pairs={{0,64},{64,128},{128,192},{192,256},{256,320},{320,384},{384,448},... | collective-permute-start | bytes 24584 | tf_op jit(solution)/shard_map/ppermute | solution.py:46
  1541.0 8.7 collective-permute-start.70
  1544.7 8.9 collective-permute-start.71
  1783.9 31.6 %collective-permute-start.72 = (f32[1,1,16,128]{3,1,2,0:T(1,128)S(1)}, f32[1,1,16,128]{3,1,2,0:T(1,128)S(1)}, u32[]{:S(2)}, u32[]{:S(2)}) collective-permute-start(f32[1,1,16,128]{3,1,2,0:T(1,128)S(1)} %get-tuple-element.125), channel_id=1, source_target_pairs={{0,64},{64,128},{128,192},{192,256},{256,320},{320,384},{384,448},... | collective-permute-start | bytes 24584 | tf_op jit(solution)/shard_map/ppermute | solution.py:46
  1951.9 8.7 collective-permute-start.82
  1955.6 8.9 collective-permute-start.83
  2194.8 31.6 %collective-permute-start.84 = (f32[1,1,16,128]{3,1,2,0:T(1,128)S(1)}, f32[1,1,16,128]{3,1,2,0:T(1,128)S(1)}, u32[]{:S(2)}, u32[]{:S(2)}) collective-permute-start(f32[1,1,16,128]{3,1,2,0:T(1,128)S(1)} %get-tuple-element.121), channel_id=1, source_target_pairs={{0,64},{64,128},{128,192},{192,256},{256,320},{320,384},{384,448},... | collective-permute-start | bytes 24584 | tf_op jit(solution)/shard_map/ppermute | solution.py:46
  2366.3 8.9 collective-permute-start.95
  (81 other events, 721.5 us)
